TPU v7x, 256 devices: a whole 4x4x8 slice. The times are simulated.
256 devices in a mesh: tok: 32 (over z_hi, x, core), lyr: 8 (over z_lo, y).
Axes of the slice: x: 4, y: 4, z: 8 (z_hi: 4, z_lo: 2; z = z_hi * 2 + z_lo), core: 2. Of those that a mesh axis runs over, the one named last changes fastest.
Arguments:
- feature_codes: bfloat16 [16, 4096, 2, 256], P('lyr', 'tok'), may hold values from 0 to 21, as said below
- block_ids: int32 [16, 4096, 2], P('lyr', 'tok'), may hold values from 0 to 31, all different within a row; in each aligned block of 128 rows (0 to 127, 128 to 255, ..., all dimensions but the last counted through in order) at most 16 rows name the same one
- target_layer: int32 [4096], P('tok'), may hold values from 0 to 15
- request_ids: int32 [4096], P('tok'), may hold values from 0 to 15
- target_resid: bfloat16 [4096, 2304], P('tok'), may hold values from -6 to 6
- decoder: bfloat16 [16, 8192, 2304], P('lyr', 'tok'), may hold values from -0.25 to 0.25
Outputs:
- scores: bfloat16 [16, 4096, 2, 256], P('lyr', 'tok')
- request_totals: float32 [16, 16, 8192], P(None, 'lyr', 'tok')
Inputs may be any that keep to these rules, and one draw needn't show every extreme that they name: `block_ids`: the 2 panel indices of one token at one source layer are distinct; among the 128 tokens of one index of tok at one source layer no panel is named by more than 16 of them, a bound that some block reaches. `feature_codes`: nonnegative, with many entries zero.
All inputs are finite; a program needn't handle non-finite values.
Results may differ from a plain program's by a relative error of at most 0.0053.
Values may be sent and summed in bfloat16 or wider, within the bound.
No kernel may reach another device: no remote copies, remote signals or barrier semaphores. Data moves between devices by JAX's collectives and lax.ppermute only.
A program may use at most 64 MiB of HBM per device.

v0:
```python
import jax
import jax.numpy as jnp
from jax import lax
from jax.sharding import PartitionSpec as P

PANELS = 32
REQUESTS = 16
CAP = 16


def slot_of(flat_ids):
    one_hot = (flat_ids[:, None] == jnp.arange(PANELS, dtype=jnp.int32)[None, :]).astype(jnp.int32)
    before = jnp.cumsum(one_hot, axis=0) - one_hot
    return flat_ids * CAP + jnp.sum(before * one_hot, axis=1)


def source_of(slot_ids):
    row_count = slot_ids.shape[0]
    empty = jnp.full((PANELS * CAP,), row_count, jnp.int32)
    return empty.at[slot_ids].set(jnp.arange(row_count, dtype=jnp.int32))


def take_rows(table, index):
    return jnp.take(table, index, axis=0)


def pad_zero(table):
    return jnp.concatenate([table, jnp.zeros((1,) + table.shape[1:], table.dtype)], axis=0)


def normalize_error(resid_rows, rebuilt):
    error = resid_rows.astype(jnp.float32) - rebuilt
    spread = jnp.mean(error * error, axis=-1, keepdims=True)
    return (error * lax.rsqrt(spread + 1e-06)).astype(jnp.bfloat16)


def per_device(feature_codes, block_ids, target_layer, request_ids, target_resid, decoder):
    layers_here, count, kact, panel = feature_codes.shape
    width = target_resid.shape[1]
    tok_count = lax.axis_size("tok")
    per_dev = PANELS // tok_count
    rows_here = count * kact
    first_layer = lax.axis_index("lyr") * layers_here
    layer_ids = first_layer + jnp.arange(layers_here, dtype=jnp.int32)
    alive_mask = (layer_ids[:, None] <= target_layer[None, :]).astype(feature_codes.dtype)
    masked = feature_codes * alive_mask[:, :, None, None]
    flat_ids = block_ids.reshape(layers_here, rows_here)
    slot_ids = jax.vmap(slot_of)(flat_ids)
    source_rows = jax.vmap(source_of)(slot_ids)
    token_of = source_rows // kact
    code_rows = jax.vmap(pad_zero)(masked.reshape(layers_here, rows_here, panel))
    send_codes = jax.vmap(take_rows)(code_rows, source_rows).reshape(
        layers_here, tok_count, per_dev, CAP, panel
    )
    panel_weights = decoder.reshape(layers_here, per_dev, panel, width)
    received = lax.all_to_all(send_codes, "tok", split_axis=1, concat_axis=1, tiled=True)
    built = jnp.einsum(
        "lspcj,lpjd->lspcd", received, panel_weights, preferred_element_type=jnp.float32
    ).astype(jnp.bfloat16)
    returned = lax.all_to_all(built, "tok", split_axis=1, concat_axis=1, tiled=True).reshape(
        layers_here, PANELS * CAP, width
    )
    per_row = jax.vmap(take_rows)(returned, slot_ids)
    partial_value = jnp.sum(
        per_row.astype(jnp.float32).reshape(layers_here, count, kact, width), axis=(0, 2)
    )
    rebuilt = lax.psum(partial_value, "lyr")
    gradient = normalize_error(target_resid, rebuilt)
    send_grad = jnp.take(pad_zero(gradient), token_of, axis=0).reshape(
        layers_here, tok_count, per_dev, CAP, width
    )
    received_grad = lax.all_to_all(send_grad, "tok", split_axis=1, concat_axis=1, tiled=True)
    projected_slots = jnp.einsum(
        "lspcd,lpjd->lspcj", received_grad, panel_weights, preferred_element_type=jnp.float32
    ).astype(jnp.bfloat16)
    coming_back = lax.all_to_all(
        projected_slots, "tok", split_axis=1, concat_axis=1, tiled=True
    ).reshape(layers_here, PANELS * CAP, panel)
    picked = jax.vmap(take_rows)(coming_back, slot_ids).reshape(layers_here, count, kact, panel)
    attribution_rows = masked.astype(jnp.float32) * picked.astype(jnp.float32)
    scores = attribution_rows.astype(jnp.bfloat16)
    members = (request_ids[:, None] == jnp.arange(REQUESTS, dtype=jnp.int32)[None, :]).astype(
        jnp.float32
    )
    panel_hot = (block_ids[..., None] == jnp.arange(PANELS, dtype=jnp.int32)).astype(jnp.float32)
    local_totals = jnp.einsum(
        "tr,ltkn,ltkj->rlnj", members, panel_hot, attribution_rows, precision=lax.Precision.HIGHEST
    )
    local_totals = local_totals.reshape(REQUESTS, layers_here, PANELS * panel)
    request_totals = lax.psum_scatter(local_totals, "tok", scatter_dimension=2, tiled=True)
    return (scores, request_totals)


def solution(mesh):
    placed = (
        P("lyr", "tok", None, None),
        P("lyr", "tok", None),
        P("tok"),
        P("tok"),
        P("tok", None),
        P("lyr", "tok", None),
    )
    return jax.shard_map(
        per_device,
        mesh=mesh,
        in_specs=placed,
        out_specs=(P("lyr", "tok", None, None), P(None, "lyr", "tok")),
        check_vma=False,
    )
```

profile of v0, /device:TPU:8, one launch (start us, length us, event | category | flops | bytes accessed | tf_op | source)
XLA Modules:
  0.0 573.8 jit_solution(13679655794225082904)
XLA Ops:
  7.2 0.0 copy-start
  7.2 1.0 copy.77
  8.1 0.1 eq.52
  8.3 0.1 reshape.172
  8.4 0.7 broadcast_multiply_fusion.1
  9.1 1.2 reduce-window.6
  10.3 0.2 slice_reduce_fusion
  10.6 0.1 copy.82
  10.7 0.0 copy-start.7
  10.7 0.0 copy-start.3
  10.8 0.1 mul.57
  10.9 0.1 fusion.30
  11.0 24.5 %scatter_fusion = s32[2,512]{1,0:T(2,128)S(1)} fusion(s32[2,512]{1,0:T(2,128)S(1)} %broadcast_in_dim.67, s32[512]{0:T(512)S(1)} %bitcast.100, s32[512]{0:T(512)S(1)} %bitcast.109), kind=kCustom, calls=%fused_computation.4 | custom fusion | bytes 10240 | tf_op jit(solution)/shard_map/vmap()/scatter | solution.py:20
  35.6 0.0 copy-done.7
  35.6 0.1 compare_convert_fusion
  35.7 0.0 copy-done.3
  35.7 0.3 broadcast_multiply_fusion
  36.1 0.4 copy.85
  36.5 0.1 broadcast_in_dim.72
  36.6 0.2 concatenate.6
  36.8 10.3 %gather_fusion.1 = bf16[1024,256]{1,0:T(8,128)(2,1)} fusion(bf16[2,257,256]{2,0,1:T(2,128)(2,1)S(1)} %concatenate.6, s32[1024]{0:T(1024)S(1)} %bitcast.99), kind=kCustom, calls=%fused_computation.1 | custom fusion | bytes 1056768 | tf_op jit(solution)/shard_map/vmap(jit(_take))/gather | solution.py:24
  47.1 1.2 copy_select_fusion.1
  48.4 28.2 %all_to_all.20 = bf16[2,32,1,16,256]{4,3,0,2,1:T(8,128)(2,1)S(1)} all-to-all(bf16[2,32,1,16,256]{4,3,0,2,1:T(8,128)(2,1)S(1)} %copy_select_fusion.1), channel_id=1, replica_groups=mesh['tok'=32,'lyr'=8] {'tok'}, dimensions={1} | all-to-all | bytes 1048576 | tf_op jit(solution)/shard_map/all_to_all | solution.py:56
  76.6 0.0 copy-done
  76.6 1.4 fusion.2
  78.0 2.7 copy.88
  80.7 5.5 all-to-all-start.1
  86.2 0.2 all-reduce.4.cloned.1.call-start
  86.5 107.6 %all-to-all-done.1 = bf16[2,32,1,16,2304]{4,3,0,2,1:T(8,128)(2,1)} async-done(((bf16[2,32,1,16,2304]{4,3,0,2,1:T(8,128)(2,1)}), bf16[2,32,1,16,2304]{4,3,0,2,1:T(8,128)(2,1)}, u32[]{:S(2)}, u32[]{:S(2)}) %all-to-all-start.1) | async-done | bytes 4718624 | tf_op jit(solution)/shard_map/all_to_all | solution.py:60
  194.1 4.9 copy.89
  199.0 13.5 %gather_fusion.2 = bf16[512,2304]{1,0:T(8,128)(2,1)} fusion(bf16[2,512,2304]{2,1,0:T(8,128)(2,1)} %bitcast.98, s32[512]{0:T(512)S(1)} %bitcast.96), kind=kCustom, calls=%fused_computation.2 | custom fusion | bytes 4722688 | tf_op jit(solution)/shard_map/vmap(jit(_take))/gather | solution.py:24
  212.4 3.7 convert_reduce_fusion
  216.2 3.8 reduce_sum.42
  219.9 5.5 reduce_sum.43
  225.5 0.0 all-reduce.4.cloned.1.call-update
  225.5 0.1 broadcast_in_dim.69
  225.6 78.2 %all-reduce.4.cloned.1.call-done = f32[128,2304]{1,0:T(8,128)} async-done(((f32[128,2304]{1,0:T(8,128)}), f32[128,2304]{1,0:T(8,128)}) %all-reduce.4.cloned.1.call-update) | async-done | bytes 1179664 | tf_op jit(solution)/shard_map/psum | solution.py:67
  303.8 0.0 copy-done.2
  303.8 1.6 multiply_reduce_fusion
  305.5 0.2 multiply_convert_fusion
  305.7 6.2 %gather_fusion = bf16[1024,2304]{1,0:T(8,128)(2,1)} fusion(bf16[129,2304]{1,0:T(8,128)(2,1)S(1)} %concatenate.7, s32[1024]{0:T(1024)S(1)} %broadcast_clamp_fusion), kind=kCustom, calls=%fused_computation | custom fusion | bytes 9441280 | tf_op jit(solution)/shard_map/jit(_take)/gather | solution.py:69
  311.9 2.8 copy_select_fusion
  314.8 99.7 %all_to_all.21 = bf16[2,32,1,16,2304]{4,3,0,2,1:T(8,128)(2,1)S(1)} all-to-all(bf16[2,32,1,16,2304]{4,3,0,2,1:T(8,128)(2,1)S(1)} %copy_select_fusion), channel_id=1, replica_groups=mesh['tok'=32,'lyr'=8] {'tok'}, dimensions={1} | all-to-all | bytes 9437184 | tf_op jit(solution)/shard_map/all_to_all | solution.py:72
  414.4 1.4 fusion.16
  415.8 0.0 copy-start.5
  415.9 0.9 copy.93
  416.7 21.7 %all-to-all-start.3 = ((bf16[2,32,1,16,256]{4,3,0,2,1:T(8,128)(2,1)}), bf16[2,32,1,16,256]{4,3,0,2,1:T(8,128)(2,1)}, u32[]{:S(2)}, u32[]{:S(2)}) async-start(bf16[2,32,1,16,256]{4,3,0,2,1:T(8,128)(2,1)} %copy.93), calls=%async_computation.3 | async-start | bytes 1048576 | tf_op jit(solution)/shard_map/all_to_all | solution.py:76
  438.4 0.3 reduce-scatter.2.cloned.1.call-start
  438.7 0.1 reduce_sum.39
  438.8 0.1 copy.80
  438.9 0.2 copy.81
  439.1 17.3 %all-to-all-done.3 = bf16[2,32,1,16,256]{4,3,0,2,1:T(8,128)(2,1)} async-done(((bf16[2,32,1,16,256]{4,3,0,2,1:T(8,128)(2,1)}), bf16[2,32,1,16,256]{4,3,0,2,1:T(8,128)(2,1)}, u32[]{:S(2)}, u32[]{:S(2)}) %all-to-all-start.3) | async-done | bytes 524320 | tf_op jit(solution)/shard_map/all_to_all | solution.py:76
  456.4 1.1 copy.94
  457.5 5.6 gather_fusion.3
  463.1 1.1 gather.28
  464.1 0.0 copy-start.6
  464.2 5.6 fusion.23
  469.7 7.5 %fusion.8 = f32[2,32,2,8,256]{4,3,2,1,0:T(8,128)S(1)} fusion(f32[2,128,256,32]{2,3,1,0:T(8,128)S(1)} %fusion.23, s32[128]{0:T(128)S(1)} %copy-done.6), kind=kOutput, calls=%fused_computation.16 | convolution fusion | flops 402655232 | bytes 9437696 | tf_op jit(solution)/shard_map/tr,ltkn,ltkj->rlnj/dot_general | solution.py:86
  477.3 1.1 copy.103
  478.4 0.0 reduce-scatter.2.cloned.1.call-update
  478.4 0.0 copy-done.4
  478.4 1.4 fusion.25
  479.8 85.7 %reduce-scatter.2.cloned.1.call-done = f32[16,2,256]{2,0,1:T(8,128)} async-done(((f32[16,2,8192]{2,0,1:T(8,128)}), f32[16,2,256]{2,0,1:T(8,128)}) %reduce-scatter.2.cloned.1.call-update) | async-done | bytes 32784 | tf_op jit(solution)/shard_map/reduce_scatter | solution.py:90
  565.5 1.4 copy.98
  (27 shorter events, 0.3 us)
Async XLA Ops:
  7.2 69.4 %copy-start = (bf16[2,256,2304]{2,1,0:T(8,128)(2,1)S(1)}, bf16[2,256,2304]{2,1,0:T(8,128)(2,1)}, u32[]{:S(2)}) copy-start(bf16[2,256,2304]{2,1,0:T(8,128)(2,1)} %param.11) | copy-start | bytes 7077892
  10.7 24.9 %copy-start.7 = (s32[128]{0:T(128)S(1)}, s32[128]{0:T(128)}, u32[]{:S(2)}) copy-start(s32[128]{0:T(128)} %param.8) | copy-start | bytes 1540
  10.7 25.0 %copy-start.3 = (bf16[2,128,2,256]{3,2,1,0:T(2,128)(2,1)S(1)}, bf16[2,128,2,256]{3,2,1,0:T(2,128)(2,1)}, u32[]{:S(2)}) copy-start(bf16[2,128,2,256]{3,2,1,0:T(2,128)(2,1)} %param.6) | copy-start | bytes 786436
  80.7 113.4 %all-to-all-start.1 = ((bf16[2,32,1,16,2304]{4,3,0,2,1:T(8,128)(2,1)}), bf16[2,32,1,16,2304]{4,3,0,2,1:T(8,128)(2,1)}, u32[]{:S(2)}, u32[]{:S(2)}) async-start(bf16[2,32,1,16,2304]{4,3,0,2,1:T(8,128)(2,1)} %copy.88), calls=%async_computation.1 | async-start | bytes 9437184 | tf_op jit(solution)/shard_map/all_to_all | solution.py:60
  86.2 217.6 %all-reduce.4.cloned.1.call-start = ((), (), s32[]{:S(2)}) async-start(), calls=%async_computation.5 | async-start | bytes 2359296 | tf_op jit(solution)/shard_map/psum | solution.py:67
  219.9 83.9 %copy-start.2 = (bf16[128,2304]{1,0:T(8,128)(2,1)S(1)}, bf16[128,2304]{1,0:T(8,128)(2,1)}, u32[]{:S(2)}) copy-start(bf16[128,2304]{1,0:T(8,128)(2,1)} %param.10) | copy-start | bytes 1769476
  303.8 1.6 copy-start.1
  415.8 23.0 %copy-start.5 = (s32[2,128,2]{1,2,0:T(2,128)S(1)}, s32[2,128,2]{1,2,0:T(2,128)}, u32[]{:S(2)}) copy-start(s32[2,128,2]{1,2,0:T(2,128)} %param.7) | copy-start | bytes 6148
  416.7 39.7 %all-to-all-start.3 = ((bf16[2,32,1,16,256]{4,3,0,2,1:T(8,128)(2,1)}), bf16[2,32,1,16,256]{4,3,0,2,1:T(8,128)(2,1)}, u32[]{:S(2)}, u32[]{:S(2)}) async-start(bf16[2,32,1,16,256]{4,3,0,2,1:T(8,128)(2,1)} %copy.93), calls=%async_computation.3 | async-start | bytes 1048576 | tf_op jit(solution)/shard_map/all_to_all | solution.py:76
  438.4 127.1 %reduce-scatter.2.cloned.1.call-start = ((), (), s32[]{:S(2)}) async-start(), calls=%async_computation.6 | async-start | bytes 1081344 | tf_op jit(solution)/shard_map/reduce_scatter | solution.py:90
  464.1 5.6 copy-start.6
  477.3 1.1 copy-start.4
Sparse Core Ops, SparseCore 0:
  225.6 78.1 all-reduce.3
  478.5 86.9 reduce-scatter.1
where the time goes:
time: 575 us; the launch traced here: 574 us
  waiting for transfers between devices  289 us (50%)
  blocking collectives  128 us (22%)
  local copies, waits for them, and re-layouts  80 us (14%)
  starting transfers between devices  27.6 us (5%)
  other arithmetic  19.1 us (3%)
  matrix products  15.9 us (3%)
  between operations  14.4 us (3%)
    all_to_all x1, waiting for transfers between devices, per_device(): lax.all_to_all(built, 'tok', split_axis=1, concat_axis=1, tiled=True)  108 us
    all_to_all x1, blocking collectives, per_device(): lax.all_to_all(send_grad, 'tok', split_axis=1, concat_axis=1, tiled=True)  99.7 us
    reduce_scatter x1, waiting for transfers between devices, per_device(): lax.psum_scatter(local_totals, 'tok', scatter_dimension=2, tiled=True)  85.7 us
    psum x1, waiting for transfers between devices, per_device(): rebuilt = lax.psum(partial_value, 'lyr')  78.2 us
    gather x4, local copies, waits for them, and re-layouts, take_rows(): return jnp.take(table, index, axis=0)  30.4 us
    all_to_all x1, blocking collectives, per_device(): lax.all_to_all(send_codes, 'tok', split_axis=1, concat_axis=1, tiled=True)  28.2 us
    scatter x1, local copies, waits for them, and re-layouts, source_of(): return empty.at[slot_ids].set(jnp.arange(row_count, dtype=jnp.int32))  24.5 us
    all_to_all x1, starting transfers between devices, per_device(): lax.all_to_all(projected_slots, 'tok', split_axis=1, concat_axis=1, tiled...  21.7 us
  transfers between devices with their start and end apart: 4, of which 4 were waited for; matrix products, arithmetic and copies ran while one was open for 0% of the time, Pallas kernels for 0%

commit v1 on v0

--- a/solution.py
+++ b/solution.py
@@ -6,6 +6,11 @@
 PANELS = 32
 REQUESTS = 16
 CAP = 16
+
+
+def add_all(x, mesh_axis):
+    parts = lax.all_gather(x, mesh_axis)
+    return jnp.sum(parts, axis=0)
 
 
 def slot_of(flat_ids):
@@ -64,7 +69,7 @@
     partial_value = jnp.sum(
         per_row.astype(jnp.float32).reshape(layers_here, count, kact, width), axis=(0, 2)
     )
-    rebuilt = lax.psum(partial_value, "lyr")
+    rebuilt = add_all(partial_value, "lyr")
     gradient = normalize_error(target_resid, rebuilt)
     send_grad = jnp.take(pad_zero(gradient), token_of, axis=0).reshape(
         layers_here, tok_count, per_dev, CAP, width

time: 575 us -> 593 us (1.031)
  waiting for transfers between devices: 289 us -> 307 us
  blocking collectives: 128 us -> 145 us
  starting transfers between devices: 27.6 us -> 12 us
  local copies, waits for them, and re-layouts: 80 us -> 73.7 us
    all_gather x0 -> x1, waiting for transfers between devices: none -> 98.7 us  [add_all(): parts = lax.all_gather(x, mesh_axis)]
    psum x1 -> x0, waiting for transfers between devices: 78.2 us -> none  [per_device(): rebuilt = lax.psum(partial_value, 'lyr')]
    all_to_all x1, blocking collectives: 99.7 us -> 117 us  [per_device(): lax.all_to_all(send_grad, 'tok', split_axis=1, concat_axis=1, tiled=True)]
    all_to_all x1, starting transfers between devices: 21.7 us -> 5.97 us  [per_device(): lax.all_to_all(projected_slots, 'tok', split_axis=1, concat_axis=1, tiled...]
    gather x4, local copies, waits for them, and re-layouts: 30.4 us -> 22.2 us  [take_rows(): return jnp.take(table, index, axis=0)]
  transfers between devices with their start and end apart: 4 -> 4, of which waited for: 4 -> 4; matrix products, arithmetic and copies ran while one was open for 0% -> 1% of each run, Pallas kernels for 0% -> 0%
where the time goes in v1:
time: 593 us; the launch traced here: 592 us
  waiting for transfers between devices  307 us (52%)
  blocking collectives  145 us (24%)
  local copies, waits for them, and re-layouts  73.7 us (12%)
  other arithmetic  23.1 us (4%)
  matrix products  16.7 us (3%)
  between operations  14.5 us (2%)
  starting transfers between devices  12 us (2%)
    all_to_all x1, blocking collectives, per_device(): lax.all_to_all(send_grad, 'tok', split_axis=1, concat_axis=1, tiled=True)  117 us
    all_to_all x1, waiting for transfers between devices, per_device(): lax.all_to_all(built, 'tok', split_axis=1, concat_axis=1, tiled=True)  108 us
    all_gather x1, waiting for transfers between devices, add_all(): parts = lax.all_gather(x, mesh_axis)  98.7 us
    reduce_scatter x1, waiting for transfers between devices, per_device(): lax.psum_scatter(local_totals, 'tok', scatter_dimension=2, tiled=True)  84.6 us
    all_to_all x1, blocking collectives, per_device(): lax.all_to_all(send_codes, 'tok', split_axis=1, concat_axis=1, tiled=True)  28.2 us
    scatter x1, local copies, waits for them, and re-layouts, source_of(): return empty.at[slot_ids].set(jnp.arange(row_count, dtype=jnp.int32))  24.5 us
    gather x4, local copies, waits for them, and re-layouts, take_rows(): return jnp.take(table, index, axis=0)  22.2 us
    all_to_all x1, waiting for transfers between devices, per_device(): lax.all_to_all(projected_slots, 'tok', split_axis=1, concat_axis=1, tiled...  15.8 us
  transfers between devices with their start and end apart: 4, of which 4 were waited for; matrix products, arithmetic and copies ran while one was open for 1% of the time, Pallas kernels for 0%

profile of v1, /device:TPU:8, one launch (start us, length us, event | category | flops | bytes accessed | tf_op | source)
XLA Modules:
  0.0 591.7 jit_solution(11829020585713474713)
XLA Ops:
  7.2 0.0 copy-start
  7.2 1.0 copy.77
  8.2 0.1 eq.52
  8.3 0.1 reshape.172
  8.4 0.7 broadcast_multiply_fusion.1
  9.1 1.2 reduce-window.6
  10.3 0.2 slice_reduce_fusion
  10.6 0.1 copy.82
  10.7 0.0 copy-start.11
  10.7 0.0 copy-start.5
  10.8 0.1 mul.57
  10.9 0.1 fusion.30
  11.1 24.5 %scatter_fusion = s32[2,512]{1,0:T(2,128)S(1)} fusion(s32[2,512]{1,0:T(2,128)S(1)} %broadcast_in_dim.67, s32[512]{0:T(512)S(1)} %bitcast.101, s32[512]{0:T(512)S(1)} %bitcast.111), kind=kCustom, calls=%fused_computation.4 | custom fusion | bytes 10240 | tf_op jit(solution)/shard_map/vmap()/scatter | solution.py:25
  35.7 0.1 compare_convert_fusion
  35.7 0.3 broadcast_multiply_fusion
  36.1 0.0 copy-start.1
  36.1 0.7 copy-done.1
  36.8 0.4 copy.85
  37.2 0.1 broadcast_in_dim.72
  37.3 0.2 concatenate.6
  37.5 5.5 gather_fusion.1
  43.0 0.2 copy_select_fusion.1
  43.2 28.2 %all_to_all.20 = bf16[2,32,1,16,256]{4,3,0,2,1:T(8,128)(2,1)S(1)} all-to-all(bf16[2,32,1,16,256]{4,3,0,2,1:T(8,128)(2,1)S(1)} %copy_select_fusion.1), channel_id=1, replica_groups=mesh['tok'=32,'lyr'=8] {'tok'}, dimensions={1} | all-to-all | bytes 1048576 | tf_op jit(solution)/shard_map/all_to_all | solution.py:61
  71.5 1.4 fusion.2
  72.9 2.7 copy.88
  75.6 5.5 all-to-all-start.1
  81.1 0.2 all-gather.3.cloned.1.call-start
  81.4 107.6 %all-to-all-done.1 = bf16[2,32,1,16,2304]{4,3,0,2,1:T(8,128)(2,1)} async-done(((bf16[2,32,1,16,2304]{4,3,0,2,1:T(8,128)(2,1)}), bf16[2,32,1,16,2304]{4,3,0,2,1:T(8,128)(2,1)}, u32[]{:S(2)}, u32[]{:S(2)}) %all-to-all-start.1) | async-done | bytes 4718624 | tf_op jit(solution)/shard_map/all_to_all | solution.py:65
  189.0 4.9 copy.89
  193.8 13.5 %gather_fusion.2 = bf16[512,2304]{1,0:T(8,128)(2,1)} fusion(bf16[2,512,2304]{2,1,0:T(8,128)(2,1)} %bitcast.99, s32[512]{0:T(512)S(1)} %bitcast.97), kind=kCustom, calls=%fused_computation.2 | custom fusion | bytes 4722688 | tf_op jit(solution)/shard_map/vmap(jit(_take))/gather | solution.py:29
  207.3 3.7 convert_reduce_fusion
  211.1 3.8 reduce_sum.51
  214.8 5.5 reduce_sum.52
  220.3 0.0 all-gather.3.cloned.1.call-update
  220.3 0.1 broadcast_in_dim.69
  220.4 0.6 copy.83
  221.0 98.7 %all-gather.3.cloned.1.call-done = f32[1024,2304]{1,0:T(8,128)} async-done(((f32[128,2304]{1,0:T(8,128)}), f32[1024,2304]{1,0:T(8,128)}) %all-gather.3.cloned.1.call-update) | async-done | bytes 9437200 | tf_op jit(solution)/shard_map/all_gather | solution.py:12
  319.7 4.4 reduce_sum.53
  324.1 1.3 multiply_reduce_fusion
  325.4 1.3 multiply_convert_fusion
  326.8 0.0 copy-start.8
  326.8 6.2 %gather_fusion = bf16[1024,2304]{1,0:T(8,128)(2,1)} fusion(bf16[129,2304]{1,0:T(8,128)(2,1)S(1)} %concatenate.7, s32[1024]{0:T(1024)S(1)} %broadcast_clamp_fusion), kind=kCustom, calls=%fused_computation | custom fusion | bytes 9441280 | tf_op jit(solution)/shard_map/jit(_take)/gather | solution.py:74
  333.0 2.8 copy_select_fusion
  335.8 116.9 %all_to_all.21 = bf16[2,32,1,16,2304]{4,3,0,2,1:T(8,128)(2,1)S(1)} all-to-all(bf16[2,32,1,16,2304]{4,3,0,2,1:T(8,128)(2,1)S(1)} %copy_select_fusion), channel_id=1, replica_groups=mesh['tok'=32,'lyr'=8] {'tok'}, dimensions={1} | all-to-all | bytes 9437184 | tf_op jit(solution)/shard_map/all_to_all | solution.py:77
  452.7 1.4 fusion.16
  454.1 0.0 copy-start.9
  454.1 0.9 copy.93
  455.0 6.0 %all-to-all-start.3 = ((bf16[2,32,1,16,256]{4,3,0,2,1:T(8,128)(2,1)}), bf16[2,32,1,16,256]{4,3,0,2,1:T(8,128)(2,1)}, u32[]{:S(2)}, u32[]{:S(2)}) async-start(bf16[2,32,1,16,256]{4,3,0,2,1:T(8,128)(2,1)} %copy.93), calls=%async_computation.3 | async-start | bytes 1048576 | tf_op jit(solution)/shard_map/all_to_all | solution.py:81
  461.0 0.3 reduce-scatter.2.cloned.1.call-start
  461.3 0.1 reduce_sum.48
  461.4 0.1 copy.80
  461.5 0.8 copy.81
  462.3 15.8 %all-to-all-done.3 = bf16[2,32,1,16,256]{4,3,0,2,1:T(8,128)(2,1)} async-done(((bf16[2,32,1,16,256]{4,3,0,2,1:T(8,128)(2,1)}), bf16[2,32,1,16,256]{4,3,0,2,1:T(8,128)(2,1)}, u32[]{:S(2)}, u32[]{:S(2)}) %all-to-all-start.3) | async-done | bytes 524320 | tf_op jit(solution)/shard_map/all_to_all | solution.py:81
  478.1 1.1 copy.94
  479.2 3.2 gather_fusion.3
  482.4 0.1 gather.28
  482.5 0.0 copy-start.10
  482.5 6.3 %fusion.23 = f32[2,128,256,32]{2,3,1,0:T(8,128)S(1)} fusion(bf16[2,128,2,256]{3,2,1,0:T(2,128)(2,1)S(1)} %copy-done.2, s32[2,128,2]{2,1,0:T(8,128)S(1)} %copy-done.4, bf16[2,128,2,256]{3,2,1,0:T(2,128)(2,1)S(1)} %gather.28, pred[2,128,2]{2,1,0:T(8,128)(4,1)} %copy.81), kind=kOutput, calls=%fused_computation.26 | convolution fusion | flops 50872320 | bytes 8915456 | tf_op jit(solution)/shard_map/tr,ltkn,ltkj->rlnj/dot_general | solution.py:91
  488.9 7.5 %fusion.8 = f32[2,32,2,8,256]{4,3,2,1,0:T(8,128)S(1)} fusion(f32[2,128,256,32]{2,3,1,0:T(8,128)S(1)} %fusion.23, s32[128]{0:T(128)S(1)} %copy-done.10), kind=kOutput, calls=%fused_computation.16 | convolution fusion | flops 402655232 | bytes 9437696 | tf_op jit(solution)/shard_map/tr,ltkn,ltkj->rlnj/dot_general | solution.py:91
  496.4 1.1 copy.103
  497.5 0.0 reduce-scatter.2.cloned.1.call-update
  497.5 1.4 fusion.25
  498.9 84.6 %reduce-scatter.2.cloned.1.call-done = f32[16,2,256]{2,0,1:T(8,128)} async-done(((f32[16,2,8192]{2,0,1:T(8,128)}), f32[16,2,256]{2,0,1:T(8,128)}) %reduce-scatter.2.cloned.1.call-update) | async-done | bytes 32784 | tf_op jit(solution)/shard_map/reduce_scatter | solution.py:95
  583.5 1.4 copy.98
  (36 shorter events, 0.3 us)
Async XLA Ops:
  7.2 64.3 %copy-start = (bf16[2,256,2304]{2,1,0:T(8,128)(2,1)S(1)}, bf16[2,256,2304]{2,1,0:T(8,128)(2,1)}, u32[]{:S(2)}) copy-start(bf16[2,256,2304]{2,1,0:T(8,128)(2,1)} %param.11) | copy-start | bytes 7077892
  8.1 2.9 copy-start.3
  10.7 24.9 %copy-start.11 = (s32[128]{0:T(128)S(1)}, s32[128]{0:T(128)}, u32[]{:S(2)}) copy-start(s32[128]{0:T(128)} %param.8) | copy-start | bytes 1540
  10.7 25.0 %copy-start.5 = (bf16[2,128,2,256]{3,2,1,0:T(2,128)(2,1)S(1)}, bf16[2,128,2,256]{3,2,1,0:T(2,128)(2,1)}, u32[]{:S(2)}) copy-start(bf16[2,128,2,256]{3,2,1,0:T(2,128)(2,1)} %param.6) | copy-start | bytes 786436
  36.1 0.7 copy-start.1
  75.6 113.4 %all-to-all-start.1 = ((bf16[2,32,1,16,2304]{4,3,0,2,1:T(8,128)(2,1)}), bf16[2,32,1,16,2304]{4,3,0,2,1:T(8,128)(2,1)}, u32[]{:S(2)}, u32[]{:S(2)}) async-start(bf16[2,32,1,16,2304]{4,3,0,2,1:T(8,128)(2,1)} %copy.88), calls=%async_computation.1 | async-start | bytes 9437184 | tf_op jit(solution)/shard_map/all_to_all | solution.py:65
  81.1 238.6 %all-gather.3.cloned.1.call-start = ((), (), s32[]{:S(2)}) async-start(), calls=%async_computation.6 | async-start | bytes 10616832 | tf_op jit(solution)/shard_map/all_gather | solution.py:12
  326.8 6.2 %copy-start.8 = (pred[2,32,16]{2,0,1:T(4,128)(4,1)S(1)}, pred[2,32,16]{2,0,1:T(4,128)(4,1)}, u32[]{:S(2)}) copy-start(pred[2,32,16]{2,0,1:T(4,128)(4,1)} %copy.83) | copy-start | bytes 3076
  454.1 7.4 %copy-start.9 = (s32[2,128,2]{1,2,0:T(2,128)S(1)}, s32[2,128,2]{1,2,0:T(2,128)}, u32[]{:S(2)}) copy-start(s32[2,128,2]{1,2,0:T(2,128)} %param.7) | copy-start | bytes 6148
  455.0 23.1 %all-to-all-start.3 = ((bf16[2,32,1,16,256]{4,3,0,2,1:T(8,128)(2,1)}), bf16[2,32,1,16,256]{4,3,0,2,1:T(8,128)(2,1)}, u32[]{:S(2)}, u32[]{:S(2)}) async-start(bf16[2,32,1,16,256]{4,3,0,2,1:T(8,128)(2,1)} %copy.93), calls=%async_computation.3 | async-start | bytes 1048576 | tf_op jit(solution)/shard_map/all_to_all | solution.py:81
  461.0 21.5 %copy-start.2 = (bf16[2,128,2,256]{3,2,1,0:T(2,128)(2,1)S(1)}, bf16[2,128,2,256]{3,2,1,0:T(2,128)(2,1)}, u32[]{:S(2)}) copy-start(bf16[2,128,2,256]{3,2,1,0:T(2,128)(2,1)} %copy-done.1) | copy-start | bytes 786436
  461.0 21.5 %copy-start.4 = (s32[2,128,2]{2,1,0:T(8,128)S(1)}, s32[2,128,2]{2,1,0:T(8,128)}, u32[]{:S(2)}) copy-start(s32[2,128,2]{2,1,0:T(8,128)} %copy-done.3) | copy-start | bytes 6148
  461.0 122.5 %reduce-scatter.2.cloned.1.call-start = ((), (), s32[]{:S(2)}) async-start(), calls=%async_computation.5 | async-start | bytes 1081344 | tf_op jit(solution)/shard_map/reduce_scatter | solution.py:95
  482.5 6.3 %copy-start.10 = (s32[128]{0:T(128)S(1)}, s32[128]{0:T(128)}, u32[]{:S(2)}) copy-start(s32[128]{0:T(128)} %param.9) | copy-start | bytes 1540
  496.4 1.1 copy-start.6
  496.4 1.1 copy-start.7
Sparse Core Ops, SparseCore 0:
  220.4 99.2 all-gather.2
  497.6 85.8 reduce-scatter.1
